TPU v7x, 256 devices: a whole 4x4x8 slice. The times are simulated.
256 devices in a mesh: expert: 64 (over y, z, core), tensor: 4 (over x).
Axes of the slice: x: 4, y: 4, z: 8, core: 2. Of those that a mesh axis runs over, the one named last changes fastest.
Arguments:
- tokens: bfloat16 [8192, 2048], P('expert', 'tensor'), may hold values from -6 to 6
- grad_out: bfloat16 [8192, 2048], P('expert', 'tensor'), may hold values from -6 to 6
- gates: float32 [8192, 6], P('expert'), may hold values from 0.1 to 1
- expert_ids: int32 [8192, 6], P('expert'), may hold values from 0 to 63, all different within a row; in each aligned block of 128 rows (0 to 127, 128 to 255, ...) at most 16 rows name the same one
- w_gate: bfloat16 [64, 2048, 1408], P('expert', None, 'tensor'), may hold values from -0.125 to 0.125
- w_up: bfloat16 [64, 2048, 1408], P('expert', None, 'tensor'), may hold values from -0.125 to 0.125
- w_down: bfloat16 [64, 1408, 2048], P('expert', 'tensor'), may hold values from -0.15625 to 0.15625
Outputs:
- mixed: bfloat16 [8192, 2048], P('expert', 'tensor')
- grad_tokens: bfloat16 [8192, 2048], P('expert', 'tensor')
- grad_gates: float32 [8192, 6], P('expert')
- grad_w_gate: bfloat16 [64, 2048, 1408], P('expert', None, 'tensor')
- grad_w_up: bfloat16 [64, 2048, 1408], P('expert', None, 'tensor')
- grad_w_down: bfloat16 [64, 1408, 2048], P('expert', 'tensor')
Inputs may be any that keep to these rules, and one draw needn't show every extreme that they name: `expert_ids`: each row names 6 different experts. In each aligned block of 128 rows (the tokens of one index of expert) no expert is named by more than 16 rows, and some block names some expert exactly 16 times.
All inputs are finite; a program needn't handle non-finite values.
Results may differ from a plain program's by a relative error of at most 0.0064.
Values may be sent and summed in bfloat16 or wider, within the bound.
A program may use at most 128 MiB of HBM per device.

v0:
```python
import jax
import jax.numpy as jnp
from jax import lax
from jax.sharding import PartitionSpec as P


def body(tokens, grad_out, gates, expert_ids, w_gate, w_up, w_down):
    expert_count = lax.axis_size("expert")
    tok_count = expert_ids.shape[0]
    top_count = expert_ids.shape[1]
    capacity = tok_count * top_count * 4 // (3 * expert_count)
    slot_total = expert_count * capacity
    flat_ids = expert_ids.reshape(-1)
    member = (flat_ids[:, None] == jnp.arange(expert_count, dtype=jnp.int32)[None, :]).astype(
        jnp.int32
    )
    earlier = jnp.cumsum(member, axis=0) - member
    position = jnp.sum(earlier * member, axis=1)
    slot_index = flat_ids * capacity + position
    pair_token = jnp.arange(tok_count * top_count, dtype=jnp.int32) // top_count
    pair_gate = gates.reshape(-1)[:, None]

    def pack(rows, scaled):
        picked = rows[pair_token]
        if scaled:
            picked = (pair_gate * picked.astype(jnp.float32)).astype(jnp.bfloat16)
        buffer = jnp.zeros((slot_total, rows.shape[1]), jnp.bfloat16).at[slot_index].set(picked)
        return buffer.reshape(expert_count, capacity, rows.shape[1])

    def dispatch(rows, scaled):
        whole = lax.all_gather(rows, "tensor", axis=1, tiled=True)
        arrived = lax.all_to_all(
            pack(whole, scaled), "expert", split_axis=0, concat_axis=0, tiled=True
        )
        return arrived.reshape(slot_total, whole.shape[1])

    def give_back(partial_value):
        shares = lax.psum_scatter(partial_value, "tensor", scatter_dimension=1, tiled=True).astype(
            jnp.bfloat16
        )
        width = shares.shape[1]
        shares = shares.reshape(expert_count, capacity, width)
        returned = lax.all_to_all(shares, "expert", split_axis=0, concat_axis=0, tiled=True)
        return returned.reshape(slot_total, width)[slot_index].reshape(tok_count, top_count, width)

    weight_gate = w_gate[0]
    weight_up = w_up[0]
    weight_down = w_down[0]
    full_rows = dispatch(tokens, False)
    gate_pre = jnp.dot(full_rows, weight_gate, preferred_element_type=jnp.float32)
    up_pre = jnp.dot(full_rows, weight_up, preferred_element_type=jnp.float32)
    sig = jax.nn.sigmoid(gate_pre)
    act = (gate_pre * sig * up_pre).astype(jnp.bfloat16)
    outputs = give_back(jnp.dot(act, weight_down, preferred_element_type=jnp.float32)).astype(
        jnp.float32
    )
    mixed = jnp.sum(gates[:, :, None] * outputs, axis=1).astype(jnp.bfloat16)
    gate_terms = jnp.sum(grad_out.astype(jnp.float32)[:, None, :] * outputs, axis=2)
    grad_gates = lax.psum(gate_terms, "tensor")
    grad_rows = dispatch(grad_out, True)
    contract_last = (((1,), (1,)), ((), ()))
    contract_first = (((0,), (0,)), ((), ()))
    grad_act = lax.dot_general(
        grad_rows, weight_down, contract_last, preferred_element_type=jnp.float32
    )
    grad_gate_pre = (grad_act * up_pre * sig * (1.0 + gate_pre * (1.0 - sig))).astype(jnp.bfloat16)
    grad_up_pre = (grad_act * gate_pre * sig).astype(jnp.bfloat16)
    grad_down = lax.dot_general(
        act, grad_rows, contract_first, preferred_element_type=jnp.float32
    ).astype(jnp.bfloat16)
    grad_gate = lax.dot_general(
        full_rows, grad_gate_pre, contract_first, preferred_element_type=jnp.float32
    ).astype(jnp.bfloat16)
    grad_up = lax.dot_general(
        full_rows, grad_up_pre, contract_first, preferred_element_type=jnp.float32
    ).astype(jnp.bfloat16)
    input_terms = lax.dot_general(
        grad_gate_pre, weight_gate, contract_last, preferred_element_type=jnp.float32
    ) + lax.dot_general(grad_up_pre, weight_up, contract_last, preferred_element_type=jnp.float32)
    input_pairs = give_back(input_terms).astype(jnp.float32)
    grad_tokens = jnp.sum(input_pairs, axis=1).astype(jnp.bfloat16)
    return (mixed, grad_tokens, grad_gates, grad_gate[None], grad_up[None], grad_down[None])


def solution(mesh):
    placed = (
        P("expert", "tensor"),
        P("expert", "tensor"),
        P("expert", None),
        P("expert", None),
        P("expert", None, "tensor"),
        P("expert", None, "tensor"),
        P("expert", "tensor", None),
    )
    return jax.shard_map(
        body,
        mesh=mesh,
        in_specs=placed,
        out_specs=(
            P("expert", "tensor"),
            P("expert", "tensor"),
            P("expert", None),
            P("expert", None, "tensor"),
            P("expert", None, "tensor"),
            P("expert", "tensor", None),
        ),
        check_vma=False,
    )
```

profile of v0, /device:TPU:32, one launch (start us, length us, event | category | flops | bytes accessed | tf_op | source)
XLA Modules:
  0.0 510.1 jit_solution(17204298319122408522)
XLA Ops:
  7.2 0.0 copy-start
  7.2 0.8 broadcast_multiply_fusion
  8.0 0.8 copy.22
  8.8 0.1 eq.29
  8.9 0.1 eq.25
  9.1 0.1 copy.21
  9.2 0.1 mul.76
  9.4 1.8 reduce-window.6
  11.2 0.3 slice_reduce_fusion
  11.5 13.3 %all_gather.6 = bf16[128,2048]{1,0:T(8,128)(2,1)S(1)} all-gather(bf16[128,512]{1,0:T(8,128)(2,1)} %param.7), channel_id=1, replica_groups=mesh['expert'=64,'tensor'=4] {'tensor'}, dimensions={1}, use_global_device_ids=true | all-gather | bytes 655360 | tf_op jit(solution)/shard_map/all_gather | solution.py:31
  24.8 0.1 fusion.22
  25.0 23.1 %scatter_custom_fusion = bf16[1024,2048]{1,0:T(8,128)(2,1)} fusion(s32[768]{0:T(1024)S(1)} %fusion.24, bf16[128,2048]{1,0:T(8,128)(2,1)S(1)} %all_gather.6, s32[1024]{0:T(1024)S(1)} %pad_clamp_fusion.1, bf16[]{:T(256)} %constant.8.clone.1), kind=kCustom, calls=%fused_computation.9 | custom fusion | bytes 4194306 | tf_op jit(solution)/shard_map/scatter | solution.py:27
  48.1 0.0 copy-start.11
  48.1 0.0 copy-start.10
  48.1 12.1 %all-to-all-start = ((bf16[64,16,2048]{2,1,0:T(8,128)(2,1)}), bf16[64,16,2048]{2,1,0:T(8,128)(2,1)}, u32[]{:S(2)}, u32[]{:S(2)}) async-start(bf16[64,16,2048]{2,1,0:T(8,128)(2,1)} %bitcast.68), calls=%async_computation | async-start | bytes 8388608 | tf_op jit(solution)/shard_map/all_to_all | solution.py:32
  60.2 0.0 copy-done.11
  60.3 0.1 copy.20
  60.4 0.6 copy-done.9
  61.0 0.1 mul.81
  61.1 0.0 copy-done.10
  61.1 12.8 %all_gather.7 = bf16[128,2048]{1,0:T(8,128)(2,1)S(1)} all-gather(bf16[128,512]{1,0:T(8,128)(2,1)S(1)} %copy-done.10), channel_id=1, replica_groups=mesh['expert'=64,'tensor'=4] {'tensor'}, dimensions={1}, use_global_device_ids=true | all-gather | bytes 655360 | tf_op jit(solution)/shard_map/all_gather | solution.py:31
  73.9 24.5 %scatter_custom_fusion.1 = bf16[1024,2048]{1,0:T(8,128)(2,1)} fusion(s32[768]{0:T(1024)S(1)} %fusion.24, f32[768]{0:T(1024)S(1)} %mul.81, bf16[]{:T(256)} %constant.8.clone.1, bf16[128,2048]{1,0:T(8,128)(2,1)S(1)} %all_gather.7, s32[1024]{0:T(1024)S(1)} %pad_clamp_fusion.1), kind=kCustom, calls=%fused_computation.8 | custom fusion | flops 4718592 | bytes 4726786 | tf_op jit(solution)/shard_map/scatter | solution.py:27
  98.4 55.6 %all-to-all-done = bf16[64,16,2048]{2,1,0:T(8,128)(2,1)} async-done(((bf16[64,16,2048]{2,1,0:T(8,128)(2,1)}), bf16[64,16,2048]{2,1,0:T(8,128)(2,1)}, u32[]{:S(2)}, u32[]{:S(2)}) %all-to-all-start) | async-done | bytes 4194336 | tf_op jit(solution)/shard_map/all_to_all | solution.py:32
  154.1 8.1 %all-to-all-start.2 = ((bf16[64,16,2048]{2,1,0:T(8,128)(2,1)}), bf16[64,16,2048]{2,1,0:T(8,128)(2,1)}, u32[]{:S(2)}, u32[]{:S(2)}) async-start(bf16[64,16,2048]{2,1,0:T(8,128)(2,1)} %bitcast.67), calls=%async_computation.3 | async-start | bytes 8388608 | tf_op jit(solution)/shard_map/all_to_all | solution.py:32
  162.2 0.0 reduce-scatter.5.cloned.1.call-start
  162.2 0.0 copy-done.3
  162.2 0.0 copy-start.4
  162.2 5.1 fusion.14
  167.3 0.0 copy-done.4
  167.3 5.0 fusion.18
  172.3 83.7 %all-to-all-done.2 = bf16[64,16,2048]{2,1,0:T(8,128)(2,1)} async-done(((bf16[64,16,2048]{2,1,0:T(8,128)(2,1)}), bf16[64,16,2048]{2,1,0:T(8,128)(2,1)}, u32[]{:S(2)}, u32[]{:S(2)}) %all-to-all-start.2) | async-done | bytes 4194336 | tf_op jit(solution)/shard_map/all_to_all | solution.py:32
  256.0 0.0 copy-done
  256.0 6.2 %multiply_convert_fusion.2 = (bf16[1024,352]{0,1:T(8,128)(2,1)S(1)}, bf16[1024,352]{0,1:T(8,128)(2,1)S(1)}, bf16[1024,352]{0,1:T(8,128)(2,1)}) fusion(f32[1024,352]{0,1:T(8,128)} %fusion.18, f32[1024,352]{0,1:T(8,128)} %fusion.14, bf16[1024,2048]{1,0:T(8,128)(2,1)} %bitcast.9, bf16[1,352,2048]{2,1,0:T(8,128)(2,1)S(1)} %copy-done), kind=kOutput, calls=%fused_computation.33 | convolution fusion | flops 1482162176 | bytes 10682368 | tf_op jit(solution)/shard_map/dot_general | solution.py:63
  262.2 0.0 copy-done.5
  262.2 2.4 fusion.16
  264.6 0.0 copy-done.6
  264.6 0.0 copy-done.1
  264.6 5.8 %convolution_add_fusion = f32[1024,2048]{1,0:T(8,128)} fusion(f32[1024,2048]{1,0:T(8,128)S(1)} %fusion.16, bf16[1024,352]{0,1:T(8,128)(2,1)S(1)} %get-tuple-element.14, bf16[1,2048,352]{1,2,0:T(8,128)(2,1)S(1)} %copy-done.3), kind=kOutput, calls=%fused_computation.7 | convolution fusion | flops 1478492160 | bytes 18939904 | tf_op jit(solution)/shard_map/dot_general | solution.py:79
  270.4 0.0 reduce-scatter.5.cloned.1.call-update
  270.4 0.3 reduce-scatter.3.cloned.1.call-start
  270.7 0.8 copy-done.8
  271.5 5.6 %fusion.11 = f32[1024,2048]{1,0:T(8,128)} fusion(bf16[1024,352]{0,1:T(8,128)(2,1)S(1)} %copy-done.8, bf16[1,352,2048]{2,1,0:T(8,128)(2,1)S(1)} %copy-done), kind=kOutput, calls=%fused_computation.24 | convolution fusion | flops 1476395008 | bytes 10551296 | tf_op jit(solution)/shard_map/dot_general | solution.py:54
  277.1 0.0 reduce-scatter.3.cloned.1.call-update
  277.1 75.1 %reduce-scatter.5.cloned.1.call-done = f32[1024,512]{1,0:T(8,128)} async-done(((f32[1024,2048]{1,0:T(8,128)}), f32[1024,512]{1,0:T(8,128)}) %reduce-scatter.5.cloned.1.call-update) | async-done | bytes 2097168 | tf_op jit(solution)/shard_map/reduce_scatter | solution.py:38
  352.2 2.7 convert_element_type.66
  354.9 10.5 %all-to-all-start.3 = ((bf16[64,16,512]{2,1,0:T(8,128)(2,1)}), bf16[64,16,512]{2,1,0:T(8,128)(2,1)S(1)}, u32[]{:S(2)}, u32[]{:S(2)}) async-start(bf16[64,16,512]{2,1,0:T(8,128)(2,1)} %bitcast.10), calls=%async_computation.5 | async-start | bytes 2097152 | tf_op jit(solution)/shard_map/all_to_all | solution.py:43
  365.4 72.3 %reduce-scatter.3.cloned.1.call-done = f32[1024,512]{1,0:T(8,128)} async-done(((f32[1024,2048]{1,0:T(8,128)}), f32[1024,512]{1,0:T(8,128)}) %reduce-scatter.3.cloned.1.call-update) | async-done | bytes 2097168 | tf_op jit(solution)/shard_map/reduce_scatter | solution.py:38
  437.7 2.7 convert_element_type.58
  440.4 0.0 all-to-all-done.3
  440.4 10.5 %all-to-all-start.1 = ((bf16[64,16,512]{2,1,0:T(8,128)(2,1)}), bf16[64,16,512]{2,1,0:T(8,128)(2,1)S(1)}, u32[]{:S(2)}, u32[]{:S(2)}) async-start(bf16[64,16,512]{2,1,0:T(8,128)(2,1)} %bitcast.69), calls=%async_computation.2 | async-start | bytes 2097152 | tf_op jit(solution)/shard_map/all_to_all | solution.py:43
  450.9 1.6 convert_element_type.67
  452.6 5.2 %fusion.4 = bf16[1,352,2048]{2,1,0:T(8,128)(2,1)} fusion(bf16[1024,352]{0,1:T(8,128)(2,1)} %get-tuple-element.16, bf16[1024,2048]{1,0:T(8,128)(2,1)} %bitcast.9), kind=kOutput, calls=%fused_computation.15 | convolution fusion | flops 1477115904 | bytes 6356992 | tf_op jit(solution)/shard_map/dot_general | solution.py:68
  457.8 5.0 fusion.6
  462.8 0.0 copy-done.7
  462.8 4.9 fusion.5
  467.8 3.3 gather_fusion.1
  471.1 1.3 reshape.153
  472.4 1.3 reduce_sum.44
  473.8 5.0 all-to-all-done.1
  478.8 3.3 gather_fusion
  482.1 1.3 reshape.154
  483.4 2.6 multiply_reduce_fusion
  486.0 16.2 %psum.7 = f32[128,6]{1,0:T(8,128)S(1)} all-reduce(f32[128,6]{1,0:T(8,128)} %get-tuple-element.12), channel_id=1, replica_groups=mesh['expert'=64,'tensor'=4] {'tensor'}, use_global_device_ids=true, to_apply=%region_10.11 | all-reduce | flops 768 | bytes 6144 | tf_op jit(solution)/shard_map/psum | solution.py:59
  502.2 0.7 copy.26
  (15 shorter events, 0.1 us)
Async XLA Ops:
  7.2 248.8 %copy-start = (bf16[1,352,2048]{2,1,0:T(8,128)(2,1)S(1)}, bf16[1,352,2048]{2,1,0:T(8,128)(2,1)}, u32[]{:S(2)}) copy-start(bf16[1,352,2048]{2,1,0:T(8,128)(2,1)} %param.13) | copy-start | bytes 4325380
  48.1 12.1 %copy-start.11 = (f32[128,6]{0,1:T(8,128)S(1)}, f32[128,6]{0,1:T(8,128)}, u32[]{:S(2)}) copy-start(f32[128,6]{0,1:T(8,128)} %param.9) | copy-start | bytes 9220
  48.1 13.0 %copy-start.10 = (bf16[128,512]{1,0:T(8,128)(2,1)S(1)}, bf16[128,512]{1,0:T(8,128)(2,1)}, u32[]{:S(2)}) copy-start(bf16[128,512]{1,0:T(8,128)(2,1)} %param.8) | copy-start | bytes 393220
  48.1 105.9 %all-to-all-start = ((bf16[64,16,2048]{2,1,0:T(8,128)(2,1)}), bf16[64,16,2048]{2,1,0:T(8,128)(2,1)}, u32[]{:S(2)}, u32[]{:S(2)}) async-start(bf16[64,16,2048]{2,1,0:T(8,128)(2,1)} %bitcast.68), calls=%async_computation | async-start | bytes 8388608 | tf_op jit(solution)/shard_map/all_to_all | solution.py:32
  60.4 0.6 copy-start.9
  154.1 8.2 %copy-start.3 = (bf16[1,2048,352]{1,2,0:T(8,128)(2,1)S(1)}, bf16[1,2048,352]{1,2,0:T(8,128)(2,1)}, u32[]{:S(2)}) copy-start(bf16[1,2048,352]{1,2,0:T(8,128)(2,1)} %param.12) | copy-start | bytes 4325380
  154.1 101.9 %all-to-all-start.2 = ((bf16[64,16,2048]{2,1,0:T(8,128)(2,1)}), bf16[64,16,2048]{2,1,0:T(8,128)(2,1)}, u32[]{:S(2)}, u32[]{:S(2)}) async-start(bf16[64,16,2048]{2,1,0:T(8,128)(2,1)} %bitcast.67), calls=%async_computation.3 | async-start | bytes 8388608 | tf_op jit(solution)/shard_map/all_to_all | solution.py:32
  162.2 190.1 %reduce-scatter.5.cloned.1.call-start = ((), (), s32[]{:S(2)}) async-start(), calls=%async_computation.7 | async-start | bytes 10485760 | tf_op jit(solution)/shard_map/reduce_scatter | solution.py:38
  162.2 5.1 copy-start.4
  256.0 6.2 %copy-start.5 = (bf16[1,2048,352]{1,2,0:T(8,128)(2,1)S(1)}, bf16[1,2048,352]{1,2,0:T(8,128)(2,1)}, u32[]{:S(2)}) copy-start(bf16[1,2048,352]{1,2,0:T(8,128)(2,1)} %param.11) | copy-start | bytes 4325380
  262.2 2.4 copy-start.6
  262.2 2.4 copy-start.1
  270.4 1.1 copy-start.8
  270.4 167.3 %reduce-scatter.3.cloned.1.call-start = ((), (), s32[]{:S(2)}) async-start(), calls=%async_computation.6 | async-start | bytes 10485760 | tf_op jit(solution)/shard_map/reduce_scatter | solution.py:38
  354.9 85.5 %all-to-all-start.3 = ((bf16[64,16,512]{2,1,0:T(8,128)(2,1)}), bf16[64,16,512]{2,1,0:T(8,128)(2,1)S(1)}, u32[]{:S(2)}, u32[]{:S(2)}) async-start(bf16[64,16,512]{2,1,0:T(8,128)(2,1)} %bitcast.10), calls=%async_computation.5 | async-start | bytes 2097152 | tf_op jit(solution)/shard_map/all_to_all | solution.py:43
  440.4 38.4 %all-to-all-start.1 = ((bf16[64,16,512]{2,1,0:T(8,128)(2,1)}), bf16[64,16,512]{2,1,0:T(8,128)(2,1)S(1)}, u32[]{:S(2)}, u32[]{:S(2)}) async-start(bf16[64,16,512]{2,1,0:T(8,128)(2,1)} %bitcast.69), calls=%async_computation.2 | async-start | bytes 2097152 | tf_op jit(solution)/shard_map/all_to_all | solution.py:43
  452.6 5.2 %copy-start.2 = (bf16[1024,352]{0,1:T(8,128)(2,1)S(1)}, bf16[1024,352]{0,1:T(8,128)(2,1)}, u32[]{:S(2)}) copy-start(bf16[1024,352]{0,1:T(8,128)(2,1)} %copy-done.1) | copy-start | bytes 2162692
  457.8 5.0 copy-start.7
Sparse Core Ops, SparseCore 0:
  270.5 81.6 reduce-scatter.4
  354.8 82.8 reduce-scatter.2
where the time goes:
time: 520 us; the launch traced here: 510 us
  waiting for transfers between devices  292 us (56%)
  matrix products  45.2 us (9%)
  blocking collectives  42.3 us (8%)
  starting transfers between devices  41.4 us (8%)
  other arithmetic  38.3 us (7%)
  local copies, waits for them, and re-layouts  36.3 us (7%)
  between operations  14.6 us (3%)
    reduce_scatter x2, waiting for transfers between devices, give_back(): lax.psum_scatter(partial_value, 'tensor', scatter_dimension=1, tiled=True)  147 us
    all_to_all x2, waiting for transfers between devices, dispatch(): lax.all_to_all(pack(whole, scaled), 'expert', split_axis=0, concat_axis=0...  139 us
    all_gather x2, blocking collectives, dispatch(): whole = lax.all_gather(rows, 'tensor', axis=1, tiled=True)  26.1 us
    scatter x1, other arithmetic, pack(): jnp.zeros((slot_total, rows.shape[1]), jnp.bfloat16).at[slot_index]  24.5 us
    scatter x1, local copies, waits for them, and re-layouts, pack(): jnp.zeros((slot_total, rows.shape[1]), jnp.bfloat16).at[slot_index]  23.1 us
    all_to_all x2, starting transfers between devices, give_back(): lax.all_to_all(shares, 'expert', split_axis=0, concat_axis=0, tiled=True)  21 us
    all_to_all x2, starting transfers between devices, dispatch(): lax.all_to_all(pack(whole, scaled), 'expert', split_axis=0, concat_axis=0...  20.2 us
    psum x1, blocking collectives, body(): grad_gates = lax.psum(gate_terms, 'tensor')  16.2 us
  transfers between devices with their start and end apart: 6, of which 5 were waited for; matrix products, arithmetic and copies ran while one was open for 13% of the time, Pallas kernels for 0%

commit v1 on v0

v1 whole, which is shorter than its diff:
```python
import functools

import jax
import jax.numpy as jnp
from jax import lax
from jax.experimental import pallas as pl
from jax.experimental.pallas import tpu as pltpu
from jax.sharding import PartitionSpec as P

F32 = jnp.float32
BF16 = jnp.bfloat16
CHUNKS = 4
AHEAD = 3
NT = (((1,), (1,)), ((), ()))
TN = (((0,), (0,)), ((), ()))


def moe_kernel(E, T, C, NC, GL, s_ref, wg_hbm, wu_hbm, wd_hbm, xg_out, act, ggp, gup, q_out, vr_out,
               xg, part, gate_s, up_s, wg, wu, wd, half_l, half_r, blk_l, blk_r, fin, vp, vx, vs,
               w_sem, out_sem, ds_sem, dr_sem, xs_sem, xr_sem, fs_sem, fr_sem, hs_sem, hr_sem,
               bs_sem, br_sem, qs_sem, qr_sem, vxs_sem, vxr_sem, vs_sem, vr_sem):
    OPC = E // NC
    CR = OPC * C
    HR = CR // 2
    W = s_ref.shape[2]
    OG = GL // C
    NG = CR // GL
    U = 2 * NC
    me = lax.axis_index("expert")
    x = lax.axis_index("tensor")
    right = lax.rem(x + 1, T)
    left = lax.rem(x + T - 1, T)
    opp = lax.rem(x + 2, T)
    xcols = pl.ds(pl.multiple_of(x * W, W), W)
    lcols = pl.ds(pl.multiple_of(left * W, W), W)
    rcols = pl.ds(pl.multiple_of(right * W, W), W)

    barrier = pltpu.get_barrier_semaphore()

    def greet(r, carry):
        pl.semaphore_signal(barrier, inc=1, device_id=(lax.rem(me + r, E), x), device_id_type=pl.DeviceIdType.MESH)
        return carry

    lax.fori_loop(1, E, greet, 0)
    for d in range(1, T):
        pl.semaphore_signal(barrier, inc=1, device_id=(me, lax.rem(x + d, T)), device_id_type=pl.DeviceIdType.MESH)
    loads = [pltpu.make_async_copy(a, b, w_sem.at[i]) for i, (a, b) in enumerate(((wg_hbm, wg), (wu_hbm, wu), (wd_hbm, wd)))]
    for load in loads:
        load.start()
    pl.semaphore_wait(barrier, E - 1 + T - 1)

    def remote(src, dst, send, recv, dev):
        return pltpu.make_async_remote_copy(src_ref=src, dst_ref=dst, send_sem=send, recv_sem=recv,
                                            device_id=dev, device_id_type=pl.DeviceIdType.MESH)

    def settle(ref, sem):
        pltpu.make_async_copy(ref, ref, sem).wait()

    def rows_of(c):
        return pl.ds(pl.multiple_of(c * CR, CR), CR)

    def first_half(c):
        return pl.ds(pl.multiple_of(c * CR, HR), HR)

    def last_half(c):
        return pl.ds(pl.multiple_of(c * CR + HR, HR), HR)

    def block(r):
        return pl.ds(pl.multiple_of(r * C, C), C)

    def dispatch(u):
        a, c = u // NC, lax.rem(u, NC)

        def one(k, carry):
            r = c * OPC + k
            to = lax.rem(me + r, E)

            @pl.when(r > 0)
            def _():
                remote(s_ref.at[a, block(to)], xg.at[a, block(r), xcols], ds_sem.at[a], dr_sem.at[u], (to, x)).start()

            @pl.when(r == 0)
            def _():
                pltpu.make_async_copy(s_ref.at[a, block(me)], xg.at[a, block(0), xcols], dr_sem.at[u]).start()

            return carry

        lax.fori_loop(0, OPC, one, 0)

    def spread(u):
        a, c = u // NC, lax.rem(u, NC)
        mine = xg.at[a, rows_of(c), xcols]
        settle(mine, dr_sem.at[u])
        remote(mine, mine, xs_sem.at[0, u], xr_sem.at[0, u], (me, right)).start()
        remote(mine, mine, xs_sem.at[1, u], xr_sem.at[1, u], (me, left)).start()

    def forward(u):
        a, c = u // NC, lax.rem(u, NC)
        settle(xg.at[a, rows_of(c), lcols], xr_sem.at[0, u])
        part_l = xg.at[a, first_half(c), lcols]
        remote(part_l, part_l, fs_sem.at[0, u], fr_sem.at[0, u], (me, right)).start()
        settle(xg.at[a, rows_of(c), rcols], xr_sem.at[1, u])
        part_r = xg.at[a, last_half(c), rcols]
        remote(part_r, part_r, fs_sem.at[1, u], fr_sem.at[1, u], (me, left)).start()

    def complete(u):
        a, c = u // NC, lax.rem(u, NC)
        ocols = pl.ds(pl.multiple_of(opp * W, W), W)
        settle(xg.at[a, first_half(c), ocols], fr_sem.at[0, u])
        settle(xg.at[a, last_half(c), ocols], fr_sem.at[1, u])
        pltpu.make_async_copy(xg.at[a, rows_of(c)], xg_out.at[a, rows_of(c)], out_sem.at[u]).start()

    def compute_forward(c):
        rows = rows_of(c)
        xc = xg[0, rows, :]
        gate = jnp.dot(xc, wg[...], preferred_element_type=F32)
        up = jnp.dot(xc, wu[...], preferred_element_type=F32)
        gate_s[rows, :] = gate
        up_s[rows, :] = up
        hidden = (gate * jax.nn.sigmoid(gate) * up).astype(BF16)
        act[rows, :] = hidden
        for q in range(T):
            part[0, q, rows, :] = jnp.dot(hidden, wd[:, q * W:(q + 1) * W], preferred_element_type=F32).astype(BF16)

    def compute_backward(c):
        rows = rows_of(c)
        grad_act = lax.dot_general(xg[1, rows, :], wd[...], NT, preferred_element_type=F32)
        gate = gate_s[rows, :]
        up = up_s[rows, :]
        sig = jax.nn.sigmoid(gate)
        term = grad_act * act[rows, :].astype(F32)
        high = term.astype(BF16)
        low = (term - high.astype(F32)).astype(BF16)
        ones = jnp.ones((8, term.shape[1]), BF16)
        sums = lax.dot_general(ones, high, NT, preferred_element_type=F32) + lax.dot_general(
            ones, low, NT, preferred_element_type=F32)
        for g in range(NG):
            vp[c * NG + g] = sums[:, g * GL:(g + 1) * GL]
        gg = (grad_act * up * sig * (1.0 + gate * (1.0 - sig))).astype(BF16)
        gu = (grad_act * gate * sig).astype(BF16)
        ggp[rows, :] = gg
        gup[rows, :] = gu
        for q in range(T):
            cut = slice(q * W, (q + 1) * W)
            part[1, q, rows, :] = (lax.dot_general(gg, wg[cut, :], NT, preferred_element_type=F32)
                                   + lax.dot_general(gu, wu[cut, :], NT, preferred_element_type=F32)).astype(BF16)

    def send_halves(w):
        a, c = w // NC, lax.rem(w, NC)
        remote(part.at[a, opp, first_half(c)], half_l.at[w], hs_sem.at[0, w], hr_sem.at[0, w], (me, right)).start()
        remote(part.at[a, opp, last_half(c)], half_r.at[w], hs_sem.at[1, w], hr_sem.at[1, w], (me, left)).start()

    def send_blocks(w):
        a, c = w // NC, lax.rem(w, NC)
        settle(half_l.at[w], hr_sem.at[0, w])
        part[a, right, first_half(c), :] = (part[a, right, first_half(c), :].astype(F32) + half_l[w].astype(F32)).astype(BF16)
        remote(part.at[a, right, rows_of(c)], blk_l.at[w], bs_sem.at[0, w], br_sem.at[0, w], (me, right)).start()
        settle(half_r.at[w], hr_sem.at[1, w])
        part[a, left, last_half(c), :] = (part[a, left, last_half(c), :].astype(F32) + half_r[w].astype(F32)).astype(BF16)
        remote(part.at[a, left, rows_of(c)], blk_r.at[w], bs_sem.at[1, w], br_sem.at[1, w], (me, left)).start()

    def give_back(w):
        a, c = w // NC, lax.rem(w, NC)
        settle(blk_l.at[w], br_sem.at[0, w])
        settle(blk_r.at[w], br_sem.at[1, w])
        fin[w] = (part[a, x, rows_of(c), :].astype(F32) + blk_l[w].astype(F32) + blk_r[w].astype(F32)).astype(BF16)

        def one(k, carry):
            r = c * OPC + k
            to = lax.rem(me - r + E, E)

            @pl.when(r > 0)
            def _():
                remote(fin.at[w, block(k)], q_out.at[a, block(me)], qs_sem.at[w], qr_sem.at[a], (to, x)).start()

            @pl.when(r == 0)
            def _():
                pltpu.make_async_copy(fin.at[w, block(0)], q_out.at[a, block(me)], qr_sem.at[a]).start()

            return carry

        lax.fori_loop(0, OPC, one, 0)

    def share_sums():
        for d in range(1, T):
            remote(vp, vx.at[d - 1], vxs_sem.at[d - 1], vxr_sem.at[d - 1], (me, lax.rem(x + d, T))).start()

    def return_sums():
        for d in range(1, T):
            settle(vx.at[d - 1], vxr_sem.at[d - 1])
        vs[...] = vp[...] + vx[0] + vx[1] + vx[2]

        def one(r, carry):
            remote(vs.at[r // OG], vr_out.at[me], vs_sem, vr_sem, (lax.rem(me - r + E, E), x)).start()
            return carry

        lax.fori_loop(1, E, one, 0)
        pltpu.make_async_copy(vs.at[0], vr_out.at[me], vr_sem).start()

    for u in range(AHEAD):
        dispatch(u)

    def step(i, carry):
        @pl.when(i + AHEAD < U)
        def _():
            dispatch(i + AHEAD)

        @pl.when(i < U)
        def _():
            spread(i)

        @pl.when(jnp.logical_and(i >= 1, i <= U))
        def _():
            forward(i - 1)

        @pl.when(jnp.logical_and(i >= U, i < 2 * U))
        def _():
            send_halves(i - U)

        @pl.when(jnp.logical_and(i >= U + 1, i <= 2 * U))
        def _():
            send_blocks(i - U - 1)

        @pl.when(i >= U + 2)
        def _():
            give_back(i - U - 2)

        @pl.when(i == U + 2)
        def _():
            return_sums()

        @pl.when(i == 2)
        def _():
            for load in loads:
                load.wait()

        @pl.when(jnp.logical_and(i >= 2, i < U + 2))
        def _():
            complete(i - 2)

        @pl.when(jnp.logical_and(i >= 2, i < NC + 2))
        def _():
            compute_forward(i - 2)

        @pl.when(jnp.logical_and(i >= NC + 2, i < U + 2))
        def _():
            compute_backward(i - 2 - NC)

        @pl.when(i == U + 1)
        def _():
            share_sums()

        return carry

    lax.fori_loop(0, 2 * U + 2, step, 0)

    def drain(u, carry):
        a, c = u // NC, lax.rem(u, NC)
        whole = fin.at[u]
        some = half_l.at[u]
        for d in range(2):
            settle(whole, xs_sem.at[d, u])
            settle(some, fs_sem.at[d, u])
            settle(some, hs_sem.at[d, u])
            settle(whole, bs_sem.at[d, u])
        settle(xg.at[a, rows_of(c)], out_sem.at[u])

        @pl.when(c > 0)
        def _():
            settle(whole, qs_sem.at[u])

        @pl.when(c == 0)
        def _():
            settle(fin.at[u, pl.ds(0, CR - C)], qs_sem.at[u])

        return carry

    lax.fori_loop(0, U, drain, 0)
    for d in range(T - 1):
        settle(vp, vxs_sem.at[d])
    settle(vr_out.at[pl.ds(0, E - 1)], vs_sem)
    settle(vr_out, vr_sem)
    for a in range(2):
        settle(s_ref.at[a, pl.ds(0, (E - 1) * C)], ds_sem.at[a])
        settle(q_out.at[a], qr_sem.at[a])


def run_kernel(E, T, C, NC, packed, w_gate, w_up, w_down):
    W = packed.shape[2]
    R = E * C
    D, FL = w_gate.shape
    CR = R // NC
    U = 2 * NC
    GL = min(128, CR)
    NG = R // GL
    dma = pltpu.SemaphoreType.DMA
    vmem = pl.BlockSpec(memory_space=pltpu.VMEM)
    hbm = pl.BlockSpec(memory_space=pl.ANY)
    flops = 2 * R * D * FL * 6
    return pl.pallas_call(
        functools.partial(moe_kernel, E, T, C, NC, GL),
        out_shape=(
            jax.ShapeDtypeStruct((2, R, D), BF16),
            jax.ShapeDtypeStruct((R, FL), BF16),
            jax.ShapeDtypeStruct((R, FL), BF16),
            jax.ShapeDtypeStruct((R, FL), BF16),
            jax.ShapeDtypeStruct((2, R, W), BF16),
            jax.ShapeDtypeStruct((E, 8, GL), F32),
        ),
        in_specs=[vmem, hbm, hbm, hbm],
        out_specs=(hbm, vmem, vmem, vmem, vmem, vmem),
        scratch_shapes=[
            pltpu.VMEM((2, R, D), BF16),
            pltpu.VMEM((2, T, R, W), BF16),
            pltpu.VMEM((R, FL), F32),
            pltpu.VMEM((R, FL), F32),
            pltpu.VMEM((D, FL), BF16),
            pltpu.VMEM((D, FL), BF16),
            pltpu.VMEM((FL, D), BF16),
            pltpu.VMEM((U, CR // 2, W), BF16),
            pltpu.VMEM((U, CR // 2, W), BF16),
            pltpu.VMEM((U, CR, W), BF16),
            pltpu.VMEM((U, CR, W), BF16),
            pltpu.VMEM((U, CR, W), BF16),
            pltpu.VMEM((NG, 8, GL), F32),
            pltpu.VMEM((T - 1, NG, 8, GL), F32),
            pltpu.VMEM((NG, 8, GL), F32),
            dma((3,)), dma((U,)), dma((2,)), dma((U,)),
            dma((2, U)), dma((2, U)), dma((2, U)), dma((2, U)), dma((2, U)), dma((2, U)),
            dma((2, U)), dma((2, U)), dma((U,)), dma((2,)),
            dma((T - 1,)), dma((T - 1,)), dma, dma,
        ],
        compiler_params=pltpu.CompilerParams(
            collective_id=0, has_side_effects=True, vmem_limit_bytes=60 * 1024 * 1024),
        cost_estimate=pl.CostEstimate(flops=flops, bytes_accessed=20 * R * D, transcendentals=2 * R * FL),
        name="moe_exchange",
    )(packed, w_gate, w_up, w_down)


def body(tokens, grad_out, gates, expert_ids, w_gate, w_up, w_down):
    E = lax.axis_size("expert")
    T = lax.axis_size("tensor")
    n, top = expert_ids.shape
    C = n * top * 4 // (3 * E)
    me = lax.axis_index("expert")
    experts = jnp.arange(E, dtype=jnp.int32)
    hit = expert_ids[:, None, :] == experts[None, :, None]
    member = jnp.any(hit, axis=2)
    gate_of = jnp.sum(jnp.where(hit, gates[:, None, :], 0.0), axis=2)
    below = (jnp.arange(n)[:, None] > jnp.arange(n)[None, :]).astype(BF16)
    earlier = jnp.dot(below, member.astype(BF16), preferred_element_type=F32).astype(jnp.int32)
    place = jnp.where(member, earlier, -1).T
    chosen = place[:, None, :] == jnp.arange(C, dtype=jnp.int32)[None, :, None]
    select = chosen.astype(BF16).reshape(E * C, n)
    weigh = jnp.where(chosen, gate_of.T[:, None, :], 0.0).reshape(E * C, n)
    slot_gate = jnp.sum(weigh, axis=1, keepdims=True)
    sent_rows = jnp.dot(select, tokens, preferred_element_type=F32).astype(BF16)
    sent_grad = (slot_gate * jnp.dot(select, grad_out, preferred_element_type=F32)).astype(BF16)
    packed = jnp.stack([sent_rows, sent_grad])
    NC = CHUNKS if E >= 64 else 2
    xg, act, ggp, gup, back, sums = run_kernel(E, T, C, NC, packed, w_gate[0], w_up[0], w_down[0])

    high = weigh.astype(BF16)
    low = (weigh - high.astype(F32)).astype(BF16)
    mixed = (lax.dot_general(high, back[0], TN, preferred_element_type=F32)
             + lax.dot_general(low, back[0], TN, preferred_element_type=F32)).astype(BF16)
    grad_tokens = lax.dot_general(select, back[1], TN, preferred_element_type=F32).astype(BF16)
    GL = sums.shape[2]
    OG = GL // C
    lane_group = lax.rem(lax.rem(experts - me + E, E), OG)
    picked = (jnp.arange(OG, dtype=jnp.int32)[None, :] == lane_group[:, None])[:, :, None]
    slot_sum = jnp.sum(jnp.where(picked, sums[:, 0, :].reshape(E, OG, C), 0.0), axis=1)
    pair_sum = jnp.sum(jnp.where(chosen, slot_sum[:, :, None], 0.0), axis=1).T
    grad_gates = jnp.sum(jnp.where(hit, pair_sum[:, :, None], 0.0), axis=1) / gates
    rows, grads = xg[0], xg[1]
    grad_down = lax.dot_general(act, grads, TN, preferred_element_type=F32).astype(BF16)
    grad_gate = lax.dot_general(rows, ggp, TN, preferred_element_type=F32).astype(BF16)
    grad_up = lax.dot_general(rows, gup, TN, preferred_element_type=F32).astype(BF16)
    return (mixed, grad_tokens, grad_gates, grad_gate[None], grad_up[None], grad_down[None])


def solution(mesh):
    placed = (
        P("expert", "tensor"),
        P("expert", "tensor"),
        P("expert", None),
        P("expert", None),
        P("expert", None, "tensor"),
        P("expert", None, "tensor"),
        P("expert", "tensor", None),
    )
    return jax.shard_map(
        body,
        mesh=mesh,
        in_specs=placed,
        out_specs=(
            P("expert", "tensor"),
            P("expert", "tensor"),
            P("expert", None),
            P("expert", None, "tensor"),
            P("expert", None, "tensor"),
            P("expert", "tensor", None),
        ),
        check_vma=False,
    )
```

time: 520 us -> 202 us (0.39); the launches traced: 510 us -> 200 us
  waiting for transfers between devices: 292 us -> 0 us
  Pallas kernels: 0 us -> 173 us
  blocking collectives: 42.3 us -> 0 us
  starting transfers between devices: 41.4 us -> 0 us
  other arithmetic: 38.3 us -> 4.57 us
  local copies, waits for them, and re-layouts: 36.3 us -> 4.84 us
  matrix products: 45.2 us -> 16.7 us
  between operations: 14.6 us -> 0.82 us
    pallas_call x0 -> x1, Pallas kernels: none -> 173 us  [run_kernel(): pl.pallas_call(functools.partial(moe_kernel, E, T, C, NC, GL), out_shape=...]
    reduce_scatter x2 -> x0, waiting for transfers between devices: 147 us -> none  [give_back(): lax.psum_scatter(partial_value, 'tensor', scatter_dimension=1, tiled=True)]
    all_to_all x4 -> x0, waiting for transfers between devices: 144 us -> none  [the longest x2 139 us: dispatch(): lax.all_to_all(pack(whole, scaled), 'expert', split_axis=0, concat_axis=0...]
    all_to_all x4 -> x0, starting transfers between devices: 41.1 us -> none  [the longest x2 21 us: give_back(): lax.all_to_all(shares, 'expert', split_axis=0, concat_axis=0, tiled=True)]
    dot_general x9, matrix products: 45.2 us -> 16.7 us  [the longest x1 5.12 us: body(): lax.dot_general(act, grads, TN, preferred_element_type=F32).astype(BF16)]
    all_gather x2 -> x0, blocking collectives: 26.1 us -> none  [dispatch(): whole = lax.all_gather(rows, 'tensor', axis=1, tiled=True)]
    scatter x1 -> x0, other arithmetic: 24.5 us -> none  [pack(): jnp.zeros((slot_total, rows.shape[1]), jnp.bfloat16).at[slot_index]]
    scatter x1 -> x0, local copies, waits for them, and re-layouts: 23.1 us -> none  [pack(): jnp.zeros((slot_total, rows.shape[1]), jnp.bfloat16).at[slot_index]]
  transfers between devices with their start and end apart: 6 -> 0, of which waited for: 5 -> 0; matrix products, arithmetic and copies ran while one was open for 13% -> 0% of each run, Pallas kernels for 0% -> 0%
where the time goes in v1:
time: 202 us; the launch traced here: 200 us
  Pallas kernels  173 us (86%)
  matrix products  16.7 us (8%)
  local copies, waits for them, and re-layouts  4.84 us (2%)
  other arithmetic  4.57 us (2%)
    pallas_call x1, Pallas kernels, run_kernel(): pl.pallas_call(functools.partial(moe_kernel, E, T, C, NC, GL), out_shape=...  173 us
    dot_general x1, matrix products, body(): lax.dot_general(act, grads, TN, preferred_element_type=F32).astype(BF16)  5.12 us

profile of v1, /device:TPU:32, one launch (start us, length us, event | category | flops | bytes accessed | tf_op | source)
XLA Modules:
  0.0 200.3 jit_solution(4983386462183193056)
XLA Ops:
  0.6 0.0 copy-start
  0.6 0.0 copy-start.4
  0.7 0.8 fusion.39
  1.4 0.1 fusion.30
  1.6 0.8 select_reduce_fusion.3
  2.3 0.2 fusion.38
  2.5 0.1 mul.10
  2.6 0.1 eq.87
  2.7 0.2 bitcast_compare_fusion
  2.9 0.0 copy-done
  2.9 0.4 fusion.27
  3.4 0.0 copy-done.4
  3.4 0.4 fusion.28
  3.8 0.0 copy-start.2
  3.8 1.6 pad_maximum_fusion.s_ref
  5.4 0.3 copy-done.2
  5.7 0.0 copy-start.3
  5.7 1.6 copy.28
  7.3 0.0 copy-done.3
  7.3 1.6 copy.29
  8.9 173.4 %moe_exchange.1 = (bf16[2,1024,2048]{2,1,0:T(8,128)(2,1)}, bf16[1024,352]{1,0:T(8,128)(2,1)}, bf16[1024,352]{1,0:T(8,128)(2,1)}, bf16[1024,352]{1,0:T(8,128)(2,1...) custom-call(bf16[2,1024,512]{2,1,0:T(8,128)(2,1)} %pad_maximum_fusion.s_ref, bf16[2048,352]{1,0:T(8,128)(2,1)} %bitcast.62, ...), custom_call_target="tpu_custom_call" | custom-call | flops 8858370048 | bytes 41943040 | tf_op jit(solution)/shard_map/moe_exchange/pallas_call | solution.py:300
  182.3 0.0 copy-start.8
  182.3 0.1 select_convert_fusion
  182.4 1.6 fusion.33
  184.1 2.2 %fusion.29 = bf16[128,512]{1,0:T(8,128)(2,1)} fusion(f32[128,512]{1,0:T(8,128)S(1)} %fusion.33, bf16[1024,128]{1,0:T(8,128)(2,1)S(1)} %bitcast.65, bf16[2,1024,512]{2,1,0:T(8,128)(2,1)} %get-tuple-element.12), kind=kOutput, calls=%fused_computation.22 | convolution fusion | flops 134348800 | bytes 1703936 | tf_op jit(solution)/shard_map/dot_general | solution.py:366
  186.3 0.0 copy-done.8
  186.3 0.0 copy-start.7
  186.3 0.0 copy-start.10
  186.3 5.1 %fusion.18 = bf16[1,352,2048]{2,1,0:T(8,128)(2,1)} fusion(bf16[1024,352]{1,0:T(8,128)(2,1)S(1)} %copy-done.8, bf16[2,1024,2048]{2,1,0:T(8,128)(2,1)} %get-tuple-element.14), kind=kOutput, calls=%fused_computation.12 | convolution fusion | flops 1477115904 | bytes 6356992 | tf_op jit(solution)/shard_map/dot_general | solution.py:376
  191.4 0.0 copy-done.7
  191.4 0.0 copy-done.10
  191.4 0.0 copy-start.9
  191.4 2.9 %fusion.21 = bf16[1,2048,352]{1,2,0:T(8,128)(2,1)} fusion(bf16[1024,352]{1,0:T(8,128)(2,1)S(1)} %copy-done.10, bf16[2,1024,2048]{2,1,0:T(8,128)(2,1)S(1)} %copy-done.7), kind=kOutput, calls=%fused_computation.13 | convolution fusion | flops 1477115904 | bytes 6422528 | tf_op jit(solution)/shard_map/dot_general | solution.py:378
  194.3 0.0 copy-done.9
  194.3 0.0 copy-start.1
  194.3 2.9 %fusion.24 = bf16[1,2048,352]{1,2,0:T(8,128)(2,1)} fusion(bf16[1024,352]{1,0:T(8,128)(2,1)S(1)} %copy-done.9, bf16[2,1024,2048]{2,1,0:T(8,128)(2,1)S(1)} %copy-done.7), kind=kOutput, calls=%fused_computation.14 | convolution fusion | flops 1477115904 | bytes 6422528 | tf_op jit(solution)/shard_map/dot_general | solution.py:377
  197.1 0.0 copy-start.5
  197.1 0.0 copy-start.6
  197.1 0.1 iota_compare_fusion
  197.2 0.0 copy-done.1
  197.2 1.0 convolution_convert_fusion.1
  198.2 1.0 slice.18
  199.2 0.1 copy.30
  199.4 0.1 copy.31
  199.4 0.2 select_reduce_fusion.1
  199.7 0.0 copy-done.5
  199.7 0.0 copy-done.6
  199.7 0.6 div.3
  (5 shorter events, 0.1 us)
Async XLA Ops:
  0.6 2.3 %copy-start = (bf16[128,512]{1,0:T(8,128)(2,1)S(1)}, bf16[128,512]{1,0:T(8,128)(2,1)}, u32[]{:S(2)}) copy-start(bf16[128,512]{1,0:T(8,128)(2,1)} %param.8) | copy-start | bytes 393220
  0.6 2.7 %copy-start.4 = (bf16[128,512]{1,0:T(8,128)(2,1)S(1)}, bf16[128,512]{1,0:T(8,128)(2,1)}, u32[]{:S(2)}) copy-start(bf16[128,512]{1,0:T(8,128)(2,1)} %param.7) | copy-start | bytes 393220
  3.8 1.9 copy-start.2
  5.7 1.6 copy-start.3
  182.3 3.9 %copy-start.8 = (bf16[1024,352]{1,0:T(8,128)(2,1)S(1)}, bf16[1024,352]{1,0:T(8,128)(2,1)}, u32[]{:S(2)}) copy-start(bf16[1024,352]{1,0:T(8,128)(2,1)} %get-tuple-element.17) | copy-start | bytes 2162692
  186.3 5.1 %copy-start.7 = (bf16[2,1024,2048]{2,1,0:T(8,128)(2,1)S(1)}, bf16[2,1024,2048]{2,1,0:T(8,128)(2,1)}, u32[]{:S(2)}) copy-start(bf16[2,1024,2048]{2,1,0:T(8,128)(2,1)} %get-tuple-element.14) | copy-start | bytes 25165828
  186.3 5.1 %copy-start.10 = (bf16[1024,352]{1,0:T(8,128)(2,1)S(1)}, bf16[1024,352]{1,0:T(8,128)(2,1)}, u32[]{:S(2)}) copy-start(bf16[1024,352]{1,0:T(8,128)(2,1)} %get-tuple-element.16) | copy-start | bytes 2162692
  191.4 2.9 %copy-start.9 = (bf16[1024,352]{1,0:T(8,128)(2,1)S(1)}, bf16[1024,352]{1,0:T(8,128)(2,1)}, u32[]{:S(2)}) copy-start(bf16[1024,352]{1,0:T(8,128)(2,1)} %get-tuple-element.15) | copy-start | bytes 2162692
  194.3 2.9 %copy-start.1 = (bf16[2,1024,512]{2,1,0:T(8,128)(2,1)S(1)}, bf16[2,1024,512]{2,1,0:T(8,128)(2,1)}, u32[]{:S(2)}) copy-start(bf16[2,1024,512]{2,1,0:T(8,128)(2,1)} %get-tuple-element.12) | copy-start | bytes 6291460
  197.1 2.6 %copy-start.5 = (s32[128,6]{0,1:T(8,128)S(1)}, s32[128,6]{0,1:T(8,128)}, u32[]{:S(2)}) copy-start(s32[128,6]{0,1:T(8,128)} %param.10) | copy-start | bytes 9220
  197.1 2.6 %copy-start.6 = (f32[128,6]{0,1:T(8,128)S(1)}, f32[128,6]{0,1:T(8,128)}, u32[]{:S(2)}) copy-start(f32[128,6]{0,1:T(8,128)} %param.9) | copy-start | bytes 9220

commit v2 on v1

v2 whole, which is shorter than its diff:
```python
import functools

import jax
import jax.numpy as jnp
from jax import lax
from jax.experimental import pallas as pl
from jax.experimental.pallas import tpu as pltpu
from jax.sharding import PartitionSpec as P

F32 = jnp.float32
BF16 = jnp.bfloat16
CHUNKS = 8
AHEAD = 8
NT = (((1,), (1,)), ((), ()))
TN = (((0,), (0,)), ((), ()))


def moe_kernel(E, T, C, NC, GL, tok_hbm, grad_hbm, gates_hbm, ids_hbm, wg_hbm, wu_hbm, wd_hbm,
               gw, mg_out, gg_out,
               tok_ref, grad_ref, gates_ref, ids_ref, s0_ref, s1_ref, place_s, gate_of_s, select_s, high_s, low_s, q1, vr,
               xg, part, q0, acts, gate_s, up_s, wg, wu, wd, half_l, half_r, blk_l, blk_r, fin, vp, vx, vs,
               in_sem, w_sem, ds_sem, dr_sem, xs_sem, xr_sem, fs_sem, fr_sem, hs_sem, hr_sem,
               bs_sem, br_sem, qs_sem, qr_sem, vxs_sem, vxr_sem, vs_sem, vr_sem):
    OPC = E // NC
    CR = OPC * C
    HR = CR // 2
    W = tok_ref.shape[1]
    OG = GL // C
    NG = CR // GL
    U = 2 * NC
    me = lax.axis_index("expert")
    x = lax.axis_index("tensor")
    right = lax.rem(x + 1, T)
    left = lax.rem(x + T - 1, T)
    opp = lax.rem(x + 2, T)
    xcols = pl.ds(pl.multiple_of(x * W, W), W)
    lcols = pl.ds(pl.multiple_of(left * W, W), W)
    rcols = pl.ds(pl.multiple_of(right * W, W), W)

    small = [pltpu.make_async_copy(a, b, in_sem.at[i]) for i, (a, b) in enumerate((
        (ids_hbm, ids_ref), (gates_hbm, gates_ref), (tok_hbm, tok_ref), (grad_hbm, grad_ref)))]
    for load in small:
        load.start()
    barrier = pltpu.get_barrier_semaphore()

    def greet(r, carry):
        pl.semaphore_signal(barrier, inc=1, device_id=(lax.rem(me + r, E), x), device_id_type=pl.DeviceIdType.MESH)
        return carry

    lax.fori_loop(1, E, greet, 0)
    for d in range(1, T):
        pl.semaphore_signal(barrier, inc=1, device_id=(me, lax.rem(x + d, T)), device_id_type=pl.DeviceIdType.MESH)
    loads = [pltpu.make_async_copy(a, b, w_sem.at[i]) for i, (a, b) in enumerate(((wg_hbm, wg), (wu_hbm, wu), (wd_hbm, wd)))]
    for load in loads:
        load.start()

    for load in small:
        load.wait()
    top, n = ids_ref.shape
    expert_row = lax.broadcasted_iota(jnp.int32, (E, n), 0)
    member = jnp.zeros((E, n), F32)
    gate_of = jnp.zeros((E, n), F32)
    for k in range(top):
        hit = ids_ref[k:k + 1, :] == expert_row
        member = member + jnp.where(hit, 1.0, 0.0)
        gate_of = gate_of + jnp.where(hit, gates_ref[k:k + 1, :], 0.0)
    ahead = jnp.where(lax.broadcasted_iota(jnp.int32, (n, n), 0) < lax.broadcasted_iota(jnp.int32, (n, n), 1), 1.0, 0.0)
    earlier = jnp.dot(member.astype(BF16), ahead.astype(BF16), preferred_element_type=F32).astype(jnp.int32)
    place_s[...] = jnp.where(member > 0.5, earlier, -1)
    gate_of_s[...] = gate_of
    BR = min(128, E * C)
    EB = BR // C

    def pack(b, carry):
        own = pl.ds(pl.multiple_of(b * EB, EB), EB)
        rows = pl.ds(pl.multiple_of(b * BR, BR), BR)
        chosen = place_s[own, :][:, None, :] == lax.broadcasted_iota(jnp.int32, (EB, C, n), 1)
        select = jnp.where(chosen, 1.0, 0.0).reshape(BR, n).astype(BF16)
        weigh = jnp.where(chosen, gate_of_s[own, :][:, None, :], 0.0).reshape(BR, n)
        high = weigh.astype(BF16)
        select_s[rows, :] = select
        high_s[rows, :] = high
        low_s[rows, :] = (weigh - high.astype(F32)).astype(BF16)
        slot_gate = jnp.sum(weigh, axis=1, keepdims=True)
        s0_ref[rows, :] = jnp.dot(select, tok_ref[...], preferred_element_type=F32).astype(BF16)
        s1_ref[rows, :] = (slot_gate * jnp.dot(select, grad_ref[...], preferred_element_type=F32)).astype(BF16)
        return carry

    lax.fori_loop(0, E * C // BR, pack, 0)
    pl.semaphore_wait(barrier, E - 1 + T - 1)

    def remote(src, dst, send, recv, dev):
        return pltpu.make_async_remote_copy(src_ref=src, dst_ref=dst, send_sem=send, recv_sem=recv,
                                            device_id=dev, device_id_type=pl.DeviceIdType.MESH)

    def settle(ref, sem):
        pltpu.make_async_copy(ref, ref, sem).wait()

    def rows_of(c):
        return pl.ds(pl.multiple_of(c * CR, CR), CR)

    def first_half(c):
        return pl.ds(pl.multiple_of(c * CR, HR), HR)

    def last_half(c):
        return pl.ds(pl.multiple_of(c * CR + HR, HR), HR)

    def block(r):
        return pl.ds(pl.multiple_of(r * C, C), C)

    def dispatch(u):
        a, c = u // NC, lax.rem(u, NC)

        def one(k, carry):
            r = c * OPC + k
            to = lax.rem(me + r, E)

            for b, s_ref in enumerate((s0_ref, s1_ref)):
                @pl.when(jnp.logical_and(a == b, r > 0))
                def _():
                    remote(s_ref.at[block(to)], xg.at[b, block(r), xcols], ds_sem.at[b], dr_sem.at[u], (to, x)).start()

                @pl.when(jnp.logical_and(a == b, r == 0))
                def _():
                    pltpu.make_async_copy(s_ref.at[block(me)], xg.at[b, block(0), xcols], dr_sem.at[u]).start()

            return carry

        lax.fori_loop(0, OPC, one, 0)

    def spread(u):
        a, c = u // NC, lax.rem(u, NC)
        mine = xg.at[a, rows_of(c), xcols]
        settle(mine, dr_sem.at[u])
        remote(mine, mine, xs_sem.at[0, u], xr_sem.at[0, u], (me, right)).start()
        remote(mine, mine, xs_sem.at[1, u], xr_sem.at[1, u], (me, left)).start()

    def forward(u):
        a, c = u // NC, lax.rem(u, NC)
        settle(xg.at[a, rows_of(c), lcols], xr_sem.at[0, u])
        part_l = xg.at[a, first_half(c), lcols]
        remote(part_l, part_l, fs_sem.at[0, u], fr_sem.at[0, u], (me, right)).start()
        settle(xg.at[a, rows_of(c), rcols], xr_sem.at[1, u])
        part_r = xg.at[a, last_half(c), rcols]
        remote(part_r, part_r, fs_sem.at[1, u], fr_sem.at[1, u], (me, left)).start()

    def complete(u):
        a, c = u // NC, lax.rem(u, NC)
        ocols = pl.ds(pl.multiple_of(opp * W, W), W)
        settle(xg.at[a, first_half(c), ocols], fr_sem.at[0, u])
        settle(xg.at[a, last_half(c), ocols], fr_sem.at[1, u])

    def compute_forward(c):
        rows = rows_of(c)
        xc = xg[0, rows, :]
        gate = lax.dot_general(wg[...], xc, NT, preferred_element_type=F32)
        up = lax.dot_general(wu[...], xc, NT, preferred_element_type=F32)
        gate_s[c] = gate
        up_s[c] = up
        hidden = gate * jax.nn.sigmoid(gate) * up
        acts[0, :, rows] = hidden.astype(BF16)
        hidden = hidden.T.astype(BF16)
        for q in range(T):
            part[0, q, rows, :] = jnp.dot(hidden, wd[:, q * W:(q + 1) * W], preferred_element_type=F32).astype(BF16)

    def compute_backward(c):
        rows = rows_of(c)
        grad_act = lax.dot_general(wd[...], xg[1, rows, :], NT, preferred_element_type=F32)
        gate = gate_s[c]
        up = up_s[c]
        sig = jax.nn.sigmoid(gate)
        sums = jnp.sum(grad_act * acts[0, :, rows].astype(F32), axis=0, keepdims=True)
        sums = jnp.broadcast_to(sums, (8, CR))
        for g in range(NG):
            vp[c * NG + g] = sums[:, g * GL:(g + 1) * GL]
        gg = grad_act * up * sig * (1.0 + gate * (1.0 - sig))
        gu = grad_act * gate * sig
        acts[1, :, rows] = gg.astype(BF16)
        acts[2, :, rows] = gu.astype(BF16)
        gg = gg.T.astype(BF16)
        gu = gu.T.astype(BF16)
        for q in range(T):
            cut = slice(q * W, (q + 1) * W)
            part[1, q, rows, :] = (jnp.dot(gg, wg[:, cut], preferred_element_type=F32)
                                   + jnp.dot(gu, wu[:, cut], preferred_element_type=F32)).astype(BF16)

    def weight_grad(j):
        m, q = j // T, lax.rem(j, T)
        cols = pl.ds(pl.multiple_of(q * W, W), W)
        a = jnp.where(m == 0, 1, 0)
        gw[m, :, cols] = jnp.dot(acts[m], xg[a, :, cols], preferred_element_type=F32).astype(BF16)

    def send_halves(w):
        a, c = w // NC, lax.rem(w, NC)
        remote(part.at[a, opp, first_half(c)], half_l.at[w], hs_sem.at[0, w], hr_sem.at[0, w], (me, right)).start()
        remote(part.at[a, opp, last_half(c)], half_r.at[w], hs_sem.at[1, w], hr_sem.at[1, w], (me, left)).start()

    def send_blocks(w):
        a, c = w // NC, lax.rem(w, NC)
        settle(half_l.at[w], hr_sem.at[0, w])
        part[a, right, first_half(c), :] = (part[a, right, first_half(c), :].astype(F32) + half_l[w].astype(F32)).astype(BF16)
        remote(part.at[a, right, rows_of(c)], blk_l.at[w], bs_sem.at[0, w], br_sem.at[0, w], (me, right)).start()
        settle(half_r.at[w], hr_sem.at[1, w])
        part[a, left, last_half(c), :] = (part[a, left, last_half(c), :].astype(F32) + half_r[w].astype(F32)).astype(BF16)
        remote(part.at[a, left, rows_of(c)], blk_r.at[w], bs_sem.at[1, w], br_sem.at[1, w], (me, left)).start()

    def give_back(w):
        a, c = w // NC, lax.rem(w, NC)
        settle(blk_l.at[w], br_sem.at[0, w])
        settle(blk_r.at[w], br_sem.at[1, w])
        fin[w] = (part[a, x, rows_of(c), :].astype(F32) + blk_l[w].astype(F32) + blk_r[w].astype(F32)).astype(BF16)

        def one(k, carry):
            r = c * OPC + k
            to = lax.rem(me - r + E, E)

            for b, q_ref in enumerate((q0, q1)):
                @pl.when(jnp.logical_and(a == b, r > 0))
                def _():
                    remote(fin.at[w, block(k)], q_ref.at[block(me)], qs_sem.at[w], qr_sem.at[b], (to, x)).start()

                @pl.when(jnp.logical_and(a == b, r == 0))
                def _():
                    pltpu.make_async_copy(fin.at[w, block(0)], q_ref.at[block(me)], qr_sem.at[b]).start()

            return carry

        lax.fori_loop(0, OPC, one, 0)

    def share_sums():
        for d in range(1, T):
            remote(vp, vx.at[d - 1], vxs_sem.at[d - 1], vxr_sem.at[d - 1], (me, lax.rem(x + d, T))).start()

    def return_sums():
        for d in range(1, T):
            settle(vx.at[d - 1], vxr_sem.at[d - 1])
        vs[...] = vp[...] + vx[0] + vx[1] + vx[2]

        def one(r, carry):
            remote(vs.at[r // OG], vr.at[me], vs_sem, vr_sem, (lax.rem(me - r + E, E), x)).start()
            return carry

        lax.fori_loop(1, E, one, 0)
        pltpu.make_async_copy(vs.at[0], vr.at[me], vr_sem).start()

    for u in range(AHEAD):
        dispatch(u)

    def step(i, carry):
        @pl.when(i + AHEAD < U)
        def _():
            dispatch(i + AHEAD)

        @pl.when(i < U)
        def _():
            spread(i)

        @pl.when(jnp.logical_and(i >= 1, i <= U))
        def _():
            forward(i - 1)

        @pl.when(jnp.logical_and(i >= U, i < 2 * U))
        def _():
            send_halves(i - U)

        @pl.when(jnp.logical_and(i >= U + 1, i <= 2 * U))
        def _():
            send_blocks(i - U - 1)

        @pl.when(jnp.logical_and(i >= U + 2, i < 2 * U + 2))
        def _():
            give_back(i - U - 2)

        @pl.when(i == U + 2)
        def _():
            return_sums()

        @pl.when(i == 2)
        def _():
            for load in loads:
                load.wait()

        @pl.when(jnp.logical_and(i >= 2, i < U + 2))
        def _():
            complete(i - 2)

        @pl.when(jnp.logical_and(i >= 2, i < NC + 2))
        def _():
            compute_forward(i - 2)

        @pl.when(jnp.logical_and(i >= NC + 2, i < U + 2))
        def _():
            compute_backward(i - 2 - NC)

        @pl.when(i == U + 1)
        def _():
            share_sums()

        @pl.when(jnp.logical_and(i >= U + 2, i < U + 2 + 3 * T))
        def _():
            weight_grad(i - U - 2)

        return carry

    lax.fori_loop(0, max(2 * U + 2, U + 2 + 3 * T), step, 0)

    def drain(u, carry):
        a, c = u // NC, lax.rem(u, NC)
        whole = fin.at[u]
        some = half_l.at[u]
        for d in range(2):
            settle(whole, xs_sem.at[d, u])
            settle(some, fs_sem.at[d, u])
            settle(some, hs_sem.at[d, u])
            settle(whole, bs_sem.at[d, u])

        @pl.when(c > 0)
        def _():
            settle(whole, qs_sem.at[u])

        @pl.when(c == 0)
        def _():
            settle(fin.at[u, pl.ds(0, CR - C)], qs_sem.at[u])

        return carry

    settle(vr.at[pl.ds(0, E - 1)], vs_sem)
    settle(vr, vr_sem)
    group = lax.rem(lax.rem(lax.broadcasted_iota(jnp.int32, (E, C), 0) - me + E, E), OG)
    sums = vr[:, 0, :]
    slot_sum = jnp.zeros((E, C), F32)
    for g in range(OG):
        slot_sum = slot_sum + jnp.where(group == g, sums[:, g * C:(g + 1) * C], 0.0)
    pair_sum = jnp.zeros((E, n), F32)
    for c in range(C):
        pair_sum = pair_sum + jnp.where(place_s[...] == c, slot_sum[:, c:c + 1], 0.0)
    for k in range(top):
        terms = jnp.where(ids_ref[k:k + 1, :] == expert_row, pair_sum, 0.0)
        gg_out[k:k + 1, :] = jnp.sum(terms, axis=0, keepdims=True) / gates_ref[k:k + 1, :]
    settle(q0, qr_sem.at[0])
    mg_out[0] = (lax.dot_general(high_s[...], q0[...], TN, preferred_element_type=F32)
                    + lax.dot_general(low_s[...], q0[...], TN, preferred_element_type=F32)).astype(BF16)
    lax.fori_loop(0, U, drain, 0)
    for d in range(T - 1):
        settle(vp, vxs_sem.at[d])
    for b, s_ref in enumerate((s0_ref, s1_ref)):
        settle(s_ref.at[pl.ds(0, (E - 1) * C)], ds_sem.at[b])
    settle(q1, qr_sem.at[1])
    mg_out[1] = lax.dot_general(select_s[...], q1[...], TN, preferred_element_type=F32).astype(BF16)


def run_kernel(E, T, C, NC, tokens, grad_out, gates, ids, w_gate, w_up, w_down):
    n, W = tokens.shape
    top = ids.shape[0]
    R = E * C
    FL, D = w_gate.shape
    CR = R // NC
    U = 2 * NC
    GL = min(128, CR)
    NG = R // GL
    dma = pltpu.SemaphoreType.DMA
    vmem = pl.BlockSpec(memory_space=pltpu.VMEM)
    hbm = pl.BlockSpec(memory_space=pltpu.HBM)
    flops = 2 * R * D * FL * 9
    return pl.pallas_call(
        functools.partial(moe_kernel, E, T, C, NC, GL),
        out_shape=(
            jax.ShapeDtypeStruct((3, FL, D), BF16),
            jax.ShapeDtypeStruct((2, n, W), BF16),
            jax.ShapeDtypeStruct((top, n), F32),
        ),
        in_specs=[hbm] * 7,
        out_specs=(vmem, vmem, vmem),
        scratch_shapes=[
            pltpu.VMEM((n, W), BF16),
            pltpu.VMEM((n, W), BF16),
            pltpu.VMEM((top, n), F32),
            pltpu.VMEM((top, n), jnp.int32),
            pltpu.VMEM((R, W), BF16),
            pltpu.VMEM((R, W), BF16),
            pltpu.VMEM((E, n), jnp.int32),
            pltpu.VMEM((E, n), F32),
            pltpu.VMEM((R, n), BF16),
            pltpu.VMEM((R, n), BF16),
            pltpu.VMEM((R, n), BF16),
            pltpu.VMEM((R, W), BF16),
            pltpu.VMEM((E, 8, GL), F32),
            pltpu.VMEM((2, R, D), BF16),
            pltpu.VMEM((2, T, R, W), BF16),
            pltpu.VMEM((R, W), BF16),
            pltpu.VMEM((3, FL, R), BF16),
            pltpu.VMEM((NC, FL, CR), F32),
            pltpu.VMEM((NC, FL, CR), F32),
            pltpu.VMEM((FL, D), BF16),
            pltpu.VMEM((FL, D), BF16),
            pltpu.VMEM((FL, D), BF16),
            pltpu.VMEM((U, CR // 2, W), BF16),
            pltpu.VMEM((U, CR // 2, W), BF16),
            pltpu.VMEM((U, CR, W), BF16),
            pltpu.VMEM((U, CR, W), BF16),
            pltpu.VMEM((U, CR, W), BF16),
            pltpu.VMEM((NG, 8, GL), F32),
            pltpu.VMEM((T - 1, NG, 8, GL), F32),
            pltpu.VMEM((NG, 8, GL), F32),
            dma((4,)), dma((3,)), dma((2,)), dma((U,)),
            dma((2, U)), dma((2, U)), dma((2, U)), dma((2, U)), dma((2, U)), dma((2, U)),
            dma((2, U)), dma((2, U)), dma((U,)), dma((2,)),
            dma((T - 1,)), dma((T - 1,)), dma, dma,
        ],
        compiler_params=pltpu.CompilerParams(
            collective_id=0, has_side_effects=True, vmem_limit_bytes=44 * 1024 * 1024),
        cost_estimate=pl.CostEstimate(flops=flops, bytes_accessed=20 * R * D, transcendentals=2 * R * FL),
        name="moe_exchange",
    )(*[pltpu.with_memory_space_constraint(a, pltpu.HBM) for a in (tokens, grad_out, gates, ids, w_gate, w_up, w_down)])


def body(tokens, grad_out, gates, expert_ids, w_gate, w_up, w_down):
    E = lax.axis_size("expert")
    T = lax.axis_size("tensor")
    n, top = expert_ids.shape
    C = n * top * 4 // (3 * E)
    NC = CHUNKS if E >= 64 else 2
    weight_grads, token_outs, grad_gates = run_kernel(
        E, T, C, NC, tokens, grad_out, gates.T, expert_ids.T, w_gate[0].T, w_up[0].T, w_down[0])
    return (token_outs[0], token_outs[1], grad_gates.T, weight_grads[1].T[None], weight_grads[2].T[None], weight_grads[0][None])


def solution(mesh):
    placed = (
        P("expert", "tensor"),
        P("expert", "tensor"),
        P("expert", None),
        P("expert", None),
        P("expert", None, "tensor"),
        P("expert", None, "tensor"),
        P("expert", "tensor", None),
    )
    return jax.shard_map(
        body,
        mesh=mesh,
        in_specs=placed,
        out_specs=(
            P("expert", "tensor"),
            P("expert", "tensor"),
            P("expert", None),
            P("expert", None, "tensor"),
            P("expert", None, "tensor"),
            P("expert", "tensor", None),
        ),
        check_vma=False,
    )
```

time: 202 us -> 176 us (0.87)
  matrix products: 16.7 us -> 0 us
  other arithmetic: 4.57 us -> 0 us
  Pallas kernels: 173 us -> 169 us
    dot_general x9 -> x0, matrix products: 16.7 us -> none  [the longest x1 5.12 us: body(): lax.dot_general(act, grads, TN, preferred_element_type=F32).astype(BF16)]
    pallas_call x1, Pallas kernels: 173 us -> 169 us  [run_kernel(): pl.pallas_call(functools.partial(moe_kernel, E, T, C, NC, GL), out_shape=...]
    unnamed x24 -> x1, local copies, waits for them, and re-layouts: 3.54 us -> 0.59 us
where the time goes in v2:
time: 176 us; the launch traced here: 173 us
  Pallas kernels  169 us (96%)
  local copies, waits for them, and re-layouts  3.52 us (2%)
    pallas_call x1, Pallas kernels, run_kernel(): pl.pallas_call(functools.partial(moe_kernel, E, T, C, NC, GL), out_shape=...  169 us

profile of v2, /device:TPU:32, one launch (start us, length us, event | category | flops | bytes accessed | tf_op | source)
XLA Modules:
  0.0 173.3 jit_solution(2371819672813610186)
XLA Ops:
  0.6 169.1 %moe_exchange.1 = (bf16[3,352,2048]{2,1,0:T(8,128)(2,1)S(1)}, bf16[2,128,512]{2,1,0:T(8,128)(2,1)S(1)}, f32[6,128]{1,0:T(8,128)S(1)}) custom-call(bf16[128,512]{1,0:T(8,128)(2,1)} %tok_hbm.1, bf16[128,512]{1,0:T(8,128)(2,1)} %grad_hbm.1, f32[6,128]{1,0:T(8,128)} %bitcast.30, s32[6,128]{1,0:T(8,128)} %bitcast.31, bf16[352,2048]{1,0:T(8,128)(2,1)} %bitcast.27, ...), custom_call_target="tpu_custom_call" | custom-call | flops 13287555072 | bytes 41943040 | tf_op jit(solution)/shard_map/moe_exchange/pallas_call | solution.py:365
  169.7 0.7 slice_bitcast_fusion.2
  170.5 2.2 %fusion = (bf16[1,352,2048]{2,1,0:T(8,128)(2,1)}, bf16[1,2048,352]{1,2,0:T(8,128)(2,1)}, bf16[1,2048,352]{1,2,0:T(8,128)(2,1)}) fusion(bf16[3,352,2048]{2,1,0:T(8,128)(2,1)S(1)} %get-tuple-element.11), kind=kLoop, calls=%fused_computation.4 | loop fusion | bytes 8650752 | tf_op jit(solution)/shard_map/slice | solution.py:425
  172.7 0.6 copy.14

commit v3 on v2

--- a/solution.py
+++ b/solution.py
@@ -10,16 +10,19 @@
 F32 = jnp.float32
 BF16 = jnp.bfloat16
 CHUNKS = 8
-AHEAD = 8
+AHEAD = 5
+CORES = 2
+NEAR = 1
+NEAR_AT = (3, 9)
 NT = (((1,), (1,)), ((), ()))
 TN = (((0,), (0,)), ((), ()))
 
 
 def moe_kernel(E, T, C, NC, GL, tok_hbm, grad_hbm, gates_hbm, ids_hbm, wg_hbm, wu_hbm, wd_hbm,
                gw, mg_out, gg_out,
-               tok_ref, grad_ref, gates_ref, ids_ref, s0_ref, s1_ref, place_s, gate_of_s, select_s, high_s, low_s, q1, vr,
+               tok_ref, grad_ref, gates_ref, ids_ref, tx, ns, slot_gate_s, s0_ref, s1_ref, place_s, gate_of_s, select_s, high_s, low_s, q1, vr,
                xg, part, q0, acts, gate_s, up_s, wg, wu, wd, half_l, half_r, blk_l, blk_r, fin, vp, vx, vs,
-               in_sem, w_sem, ds_sem, dr_sem, xs_sem, xr_sem, fs_sem, fr_sem, hs_sem, hr_sem,
+               in_sem, ts_sem, tr_sem, tf_sem, tg_sem, ns_sem, w_sem, ds_sem, dr_sem, xs_sem, xr_sem, fs_sem, fr_sem, hs_sem, hr_sem,
                bs_sem, br_sem, qs_sem, qr_sem, vxs_sem, vxr_sem, vs_sem, vr_sem):
     OPC = E // NC
     CR = OPC * C
@@ -38,13 +41,39 @@
     rcols = pl.ds(pl.multiple_of(right * W, W), W)
 
     small = [pltpu.make_async_copy(a, b, in_sem.at[i]) for i, (a, b) in enumerate((
-        (ids_hbm, ids_ref), (gates_hbm, gates_ref), (tok_hbm, tok_ref), (grad_hbm, grad_ref)))]
+        (ids_hbm, ids_ref), (gates_hbm, gates_ref), (tok_hbm, tok_ref), (grad_hbm, grad_ref),
+        (tok_hbm, tx.at[0, :, xcols]), (grad_hbm, tx.at[1, :, xcols])))]
     for load in small:
         load.start()
     barrier = pltpu.get_barrier_semaphore()
-
-    def greet(r, carry):
-        pl.semaphore_signal(barrier, inc=1, device_id=(lax.rem(me + r, E), x), device_id_type=pl.DeviceIdType.MESH)
+    Y = OPC // CORES
+    my_y = me // (NC * CORES)
+    my_z = lax.rem(me // CORES, NC)
+    my_core = lax.rem(me, CORES)
+
+    order = sorted(range(NC), key=lambda d: (min(d, NC - d) * 2 + (2 * d <= NC)))
+    near = [0, NC - 1][:NEAR]
+    order = [d for d in order if d not in near] + near[::-1]
+    FAR = NC - NEAR
+    SELF = (NC - 1) * OPC
+
+    def offset(c, k):
+        dz = sum(jnp.where(c == i, d, 0) for i, d in enumerate(order))
+        return k // CORES, dz, lax.rem(k, CORES)
+
+    def expert_at(c, k):
+        dy, dz, dc = offset(c, k)
+        return (lax.rem(my_y + dy, Y) * NC + lax.rem(my_z + dz, NC)) * CORES + lax.rem(my_core + dc, CORES)
+
+    def source_at(c, k):
+        dy, dz, dc = offset(c, k)
+        return ((lax.rem(my_y - dy + Y, Y) * NC + lax.rem(my_z - dz + NC, NC)) * CORES
+                + lax.rem(my_core - dc + CORES, CORES))
+
+    def greet(i, carry):
+        r = lax.rem(i + SELF, E)
+        pl.semaphore_signal(barrier, inc=1, device_id=(expert_at(r // OPC, lax.rem(r, OPC)), x),
+                            device_id_type=pl.DeviceIdType.MESH)
         return carry
 
     lax.fori_loop(1, E, greet, 0)
@@ -76,13 +105,21 @@
         rows = pl.ds(pl.multiple_of(b * BR, BR), BR)
         chosen = place_s[own, :][:, None, :] == lax.broadcasted_iota(jnp.int32, (EB, C, n), 1)
         select = jnp.where(chosen, 1.0, 0.0).reshape(BR, n).astype(BF16)
+        select_s[rows, :] = select
+        s0_ref[rows, :] = jnp.dot(select, tok_ref[...], preferred_element_type=F32).astype(BF16)
+        return carry
+
+    def pack_grad(b, carry):
+        own = pl.ds(pl.multiple_of(b * EB, EB), EB)
+        rows = pl.ds(pl.multiple_of(b * BR, BR), BR)
+        chosen = place_s[own, :][:, None, :] == lax.broadcasted_iota(jnp.int32, (EB, C, n), 1)
+        select = select_s[rows, :]
         weigh = jnp.where(chosen, gate_of_s[own, :][:, None, :], 0.0).reshape(BR, n)
         high = weigh.astype(BF16)
-        select_s[rows, :] = select
         high_s[rows, :] = high
         low_s[rows, :] = (weigh - high.astype(F32)).astype(BF16)
         slot_gate = jnp.sum(weigh, axis=1, keepdims=True)
-        s0_ref[rows, :] = jnp.dot(select, tok_ref[...], preferred_element_type=F32).astype(BF16)
+        slot_gate_s[rows, :] = slot_gate
         s1_ref[rows, :] = (slot_gate * jnp.dot(select, grad_ref[...], preferred_element_type=F32)).astype(BF16)
         return carry
 
@@ -113,42 +150,103 @@
 
         def one(k, carry):
             r = c * OPC + k
-            to = lax.rem(me + r, E)
-
+            to = expert_at(c, k)
             for b, s_ref in enumerate((s0_ref, s1_ref)):
-                @pl.when(jnp.logical_and(a == b, r > 0))
+                @pl.when(a == b)
                 def _():
                     remote(s_ref.at[block(to)], xg.at[b, block(r), xcols], ds_sem.at[b], dr_sem.at[u], (to, x)).start()
 
-                @pl.when(jnp.logical_and(a == b, r == 0))
-                def _():
-                    pltpu.make_async_copy(s_ref.at[block(me)], xg.at[b, block(0), xcols], dr_sem.at[u]).start()
-
             return carry
 
-        lax.fori_loop(0, OPC, one, 0)
+        @pl.when(c < FAR)
+        def _():
+            lax.fori_loop(0, OPC, one, 0)
+
+    HN = n // 2
+
+    def gather_start():
+        for a in range(2):
+            mine = tx.at[a, :, xcols]
+            remote(mine, mine, ts_sem.at[0, a], tr_sem.at[0, a], (me, right)).start()
+            remote(mine, mine, ts_sem.at[1, a], tr_sem.at[1, a], (me, left)).start()
+
+    def gather_forward():
+        for a in range(2):
+            settle(tx.at[a, :, lcols], tr_sem.at[0, a])
+            part_l = tx.at[a, pl.ds(0, HN), lcols]
+            remote(part_l, part_l, tf_sem.at[0, a], tg_sem.at[0, a], (me, right)).start()
+            settle(tx.at[a, :, rcols], tr_sem.at[1, a])
+            part_r = tx.at[a, pl.ds(HN, HN), rcols]
+            remote(part_r, part_r, tf_sem.at[1, a], tg_sem.at[1, a], (me, left)).start()
+
+    def pack_near():
+        ocols = pl.ds(pl.multiple_of(opp * W, W), W)
+        for a in range(2):
+            settle(tx.at[a, pl.ds(0, HN), ocols], tg_sem.at[0, a])
+            settle(tx.at[a, pl.ds(HN, HN), ocols], tg_sem.at[1, a])
+
+        def fill(j, carry):
+            to = expert_at(FAR + j // OPC, lax.rem(j, OPC))
+            select = select_s[block(to), :]
+            ns[0, block(j), :] = jnp.dot(select, tx[0], preferred_element_type=F32).astype(BF16)
+            scaled = slot_gate_s[block(to), :] * jnp.dot(select, tx[1], preferred_element_type=F32)
+            ns[1, block(j), :] = scaled.astype(BF16)
+            return carry
+
+        lax.fori_loop(0, NEAR * OPC, fill, 0)
+
+    def dispatch_near(a):
+        def one(j, carry):
+            c = FAR + j // OPC
+            r = FAR * OPC + j
+            to = expert_at(c, lax.rem(j, OPC))
+
+            @pl.when(r != SELF)
+            def _():
+                remote(ns.at[a, block(j)], xg.at[a, block(r)], ns_sem.at[a], dr_sem.at[a * NC + c], (to, x)).start()
+
+            @pl.when(r == SELF)
+            def _():
+                pltpu.make_async_copy(ns.at[a, block(j)], xg.at[a, block(r)], dr_sem.at[a * NC + c]).start()
+
+            return carry
+
+        lax.fori_loop(0, NEAR * OPC, one, 0)
 
     def spread(u):
         a, c = u // NC, lax.rem(u, NC)
-        mine = xg.at[a, rows_of(c), xcols]
-        settle(mine, dr_sem.at[u])
-        remote(mine, mine, xs_sem.at[0, u], xr_sem.at[0, u], (me, right)).start()
-        remote(mine, mine, xs_sem.at[1, u], xr_sem.at[1, u], (me, left)).start()
+
+        @pl.when(c < FAR)
+        def _():
+            mine = xg.at[a, rows_of(c), xcols]
+            settle(mine, dr_sem.at[u])
+            remote(mine, mine, xs_sem.at[0, u], xr_sem.at[0, u], (me, right)).start()
+            remote(mine, mine, xs_sem.at[1, u], xr_sem.at[1, u], (me, left)).start()
 
     def forward(u):
         a, c = u // NC, lax.rem(u, NC)
-        settle(xg.at[a, rows_of(c), lcols], xr_sem.at[0, u])
-        part_l = xg.at[a, first_half(c), lcols]
-        remote(part_l, part_l, fs_sem.at[0, u], fr_sem.at[0, u], (me, right)).start()
-        settle(xg.at[a, rows_of(c), rcols], xr_sem.at[1, u])
-        part_r = xg.at[a, last_half(c), rcols]
-        remote(part_r, part_r, fs_sem.at[1, u], fr_sem.at[1, u], (me, left)).start()
+
+        @pl.when(c < FAR)
+        def _():
+            settle(xg.at[a, rows_of(c), lcols], xr_sem.at[0, u])
+            part_l = xg.at[a, first_half(c), lcols]
+            remote(part_l, part_l, fs_sem.at[0, u], fr_sem.at[0, u], (me, right)).start()
+            settle(xg.at[a, rows_of(c), rcols], xr_sem.at[1, u])
+            part_r = xg.at[a, last_half(c), rcols]
+            remote(part_r, part_r, fs_sem.at[1, u], fr_sem.at[1, u], (me, left)).start()
 
     def complete(u):
         a, c = u // NC, lax.rem(u, NC)
-        ocols = pl.ds(pl.multiple_of(opp * W, W), W)
-        settle(xg.at[a, first_half(c), ocols], fr_sem.at[0, u])
-        settle(xg.at[a, last_half(c), ocols], fr_sem.at[1, u])
+
+        @pl.when(c < FAR)
+        def _():
+            ocols = pl.ds(pl.multiple_of(opp * W, W), W)
+            settle(xg.at[a, first_half(c), ocols], fr_sem.at[0, u])
+            settle(xg.at[a, last_half(c), ocols], fr_sem.at[1, u])
+
+        @pl.when(c >= FAR)
+        def _():
+            settle(xg.at[a, rows_of(c)], dr_sem.at[u])
 
     def compute_forward(c):
         rows = rows_of(c)
@@ -190,13 +288,17 @@
         a = jnp.where(m == 0, 1, 0)
         gw[m, :, cols] = jnp.dot(acts[m], xg[a, :, cols], preferred_element_type=F32).astype(BF16)
 
+    def return_chunk(w):
+        p = lax.rem(w, NC)
+        return jnp.where(p < FAR, FAR - 1 - p, p)
+
     def send_halves(w):
-        a, c = w // NC, lax.rem(w, NC)
+        a, c = w // NC, return_chunk(w)
         remote(part.at[a, opp, first_half(c)], half_l.at[w], hs_sem.at[0, w], hr_sem.at[0, w], (me, right)).start()
         remote(part.at[a, opp, last_half(c)], half_r.at[w], hs_sem.at[1, w], hr_sem.at[1, w], (me, left)).start()
 
     def send_blocks(w):
-        a, c = w // NC, lax.rem(w, NC)
+        a, c = w // NC, return_chunk(w)
         settle(half_l.at[w], hr_sem.at[0, w])
         part[a, right, first_half(c), :] = (part[a, right, first_half(c), :].astype(F32) + half_l[w].astype(F32)).astype(BF16)
         remote(part.at[a, right, rows_of(c)], blk_l.at[w], bs_sem.at[0, w], br_sem.at[0, w], (me, right)).start()
@@ -205,23 +307,23 @@
         remote(part.at[a, left, rows_of(c)], blk_r.at[w], bs_sem.at[1, w], br_sem.at[1, w], (me, left)).start()
 
     def give_back(w):
-        a, c = w // NC, lax.rem(w, NC)
+        a, c = w // NC, return_chunk(w)
         settle(blk_l.at[w], br_sem.at[0, w])
         settle(blk_r.at[w], br_sem.at[1, w])
         fin[w] = (part[a, x, rows_of(c), :].astype(F32) + blk_l[w].astype(F32) + blk_r[w].astype(F32)).astype(BF16)
 
         def one(k, carry):
             r = c * OPC + k
-            to = lax.rem(me - r + E, E)
+            to = source_at(c, k)
 
             for b, q_ref in enumerate((q0, q1)):
-                @pl.when(jnp.logical_and(a == b, r > 0))
+                @pl.when(jnp.logical_and(a == b, r != SELF))
                 def _():
                     remote(fin.at[w, block(k)], q_ref.at[block(me)], qs_sem.at[w], qr_sem.at[b], (to, x)).start()
 
-                @pl.when(jnp.logical_and(a == b, r == 0))
+                @pl.when(jnp.logical_and(a == b, r == SELF))
                 def _():
-                    pltpu.make_async_copy(fin.at[w, block(0)], q_ref.at[block(me)], qr_sem.at[b]).start()
+                    pltpu.make_async_copy(fin.at[w, block(k)], q_ref.at[block(me)], qr_sem.at[b]).start()
 
             return carry
 
@@ -236,20 +338,24 @@
             settle(vx.at[d - 1], vxr_sem.at[d - 1])
         vs[...] = vp[...] + vx[0] + vx[1] + vx[2]
 
-        def one(r, carry):
-            remote(vs.at[r // OG], vr.at[me], vs_sem, vr_sem, (lax.rem(me - r + E, E), x)).start()
+        def one(i, carry):
+            r = lax.rem(i + SELF, E)
+            remote(vs.at[r // OG], vr.at[me], vs_sem, vr_sem, (source_at(r // OPC, lax.rem(r, OPC)), x)).start()
             return carry
 
         lax.fori_loop(1, E, one, 0)
-        pltpu.make_async_copy(vs.at[0], vr.at[me], vr_sem).start()
-
-    for u in range(AHEAD):
+        pltpu.make_async_copy(vs.at[SELF // OG], vr.at[me], vr_sem).start()
+
+    gather_start()
+    for u in range(min(AHEAD, FAR)):
         dispatch(u)
+    lax.fori_loop(0, E * C // BR, pack_grad, 0)
+    gather_forward()
 
     def step(i, carry):
-        @pl.when(i + AHEAD < U)
-        def _():
-            dispatch(i + AHEAD)
+        @pl.when(i + min(AHEAD, FAR) < U)
+        def _():
+            dispatch(i + min(AHEAD, FAR))
 
         @pl.when(i < U)
         def _():
@@ -258,6 +364,15 @@
         @pl.when(jnp.logical_and(i >= 1, i <= U))
         def _():
             forward(i - 1)
+
+        @pl.when(i == 1)
+        def _():
+            pack_near()
+
+        for a, when in enumerate(NEAR_AT):
+            @pl.when(i == min(when, (a + 1) * NC))
+            def _():
+                dispatch_near(a)
 
         @pl.when(jnp.logical_and(i >= U, i < 2 * U))
         def _():
@@ -305,20 +420,24 @@
     lax.fori_loop(0, max(2 * U + 2, U + 2 + 3 * T), step, 0)
 
     def drain(u, carry):
-        a, c = u // NC, lax.rem(u, NC)
+        a, c = u // NC, return_chunk(u)
         whole = fin.at[u]
         some = half_l.at[u]
+        @pl.when(lax.rem(u, NC) < FAR)
+        def _():
+            for d in range(2):
+                settle(whole, xs_sem.at[d, u])
+                settle(some, fs_sem.at[d, u])
+
         for d in range(2):
-            settle(whole, xs_sem.at[d, u])
-            settle(some, fs_sem.at[d, u])
             settle(some, hs_sem.at[d, u])
             settle(whole, bs_sem.at[d, u])
 
-        @pl.when(c > 0)
+        @pl.when(c != NC - 1)
         def _():
             settle(whole, qs_sem.at[u])
 
-        @pl.when(c == 0)
+        @pl.when(c == NC - 1)
         def _():
             settle(fin.at[u, pl.ds(0, CR - C)], qs_sem.at[u])
 
@@ -326,7 +445,9 @@
 
     settle(vr.at[pl.ds(0, E - 1)], vs_sem)
     settle(vr, vr_sem)
-    group = lax.rem(lax.rem(lax.broadcasted_iota(jnp.int32, (E, C), 0) - me + E, E), OG)
+    expert = lax.broadcasted_iota(jnp.int32, (E, C), 0)
+    away_y = lax.rem(lax.div(expert, NC * CORES) - my_y + Y, Y)
+    group = away_y * CORES + lax.rem(lax.rem(expert, CORES) - my_core + CORES, CORES)
     sums = vr[:, 0, :]
     slot_sum = jnp.zeros((E, C), F32)
     for g in range(OG):
@@ -344,7 +465,11 @@
     for d in range(T - 1):
         settle(vp, vxs_sem.at[d])
     for b, s_ref in enumerate((s0_ref, s1_ref)):
-        settle(s_ref.at[pl.ds(0, (E - 1) * C)], ds_sem.at[b])
+        settle(s_ref.at[pl.ds(0, FAR * CR)], ds_sem.at[b])
+        settle(ns.at[b, pl.ds(0, NEAR * CR - C)], ns_sem.at[b])
+        for d in range(2):
+            settle(tx.at[b, :, xcols], ts_sem.at[d, b])
+            settle(tx.at[b, pl.ds(0, HN), xcols], tf_sem.at[d, b])
     settle(q1, qr_sem.at[1])
     mg_out[1] = lax.dot_general(select_s[...], q1[...], TN, preferred_element_type=F32).astype(BF16)
 
@@ -376,6 +501,9 @@
             pltpu.VMEM((n, W), BF16),
             pltpu.VMEM((top, n), F32),
             pltpu.VMEM((top, n), jnp.int32),
+            pltpu.VMEM((2, n, D), BF16),
+            pltpu.VMEM((2, NEAR * CR, D), BF16),
+            pltpu.VMEM((R, 1), F32),
             pltpu.VMEM((R, W), BF16),
             pltpu.VMEM((R, W), BF16),
             pltpu.VMEM((E, n), jnp.int32),
@@ -402,7 +530,7 @@
             pltpu.VMEM((NG, 8, GL), F32),
             pltpu.VMEM((T - 1, NG, 8, GL), F32),
             pltpu.VMEM((NG, 8, GL), F32),
-            dma((4,)), dma((3,)), dma((2,)), dma((U,)),
+            dma((6,)), dma((2, 2)), dma((2, 2)), dma((2, 2)), dma((2, 2)), dma((2,)), dma((3,)), dma((2,)), dma((U,)),
             dma((2, U)), dma((2, U)), dma((2, U)), dma((2, U)), dma((2, U)), dma((2, U)),
             dma((2, U)), dma((2, U)), dma((U,)), dma((2,)),
             dma((T - 1,)), dma((T - 1,)), dma, dma,

time: 176 us -> 173 us (0.983)
  Pallas kernels: 169 us -> 167 us
where the time goes in v3:
time: 173 us; the launch traced here: 172 us
  Pallas kernels  167 us (97%)
  local copies, waits for them, and re-layouts  3.52 us (2%)
    pallas_call x1, Pallas kernels, run_kernel(): pl.pallas_call(functools.partial(moe_kernel, E, T, C, NC, GL), out_shape=...  167 us

profile of v3, /device:TPU:32, one launch (start us, length us, event | category | flops | bytes accessed | tf_op | source)
XLA Modules:
  0.0 171.6 jit_solution(2070325331245914348)
XLA Ops:
  0.6 167.4 %moe_exchange.1 = (bf16[3,352,2048]{2,1,0:T(8,128)(2,1)S(1)}, bf16[2,128,512]{2,1,0:T(8,128)(2,1)S(1)}, f32[6,128]{1,0:T(8,128)S(1)}) custom-call(bf16[128,512]{1,0:T(8,128)(2,1)} %tok_hbm.1, bf16[128,512]{1,0:T(8,128)(2,1)} %grad_hbm.1, f32[6,128]{1,0:T(8,128)} %bitcast.30, s32[6,128]{1,0:T(8,128)} %bitcast.31, bf16[352,2048]{1,0:T(8,128)(2,1)} %bitcast.27, ...), custom_call_target="tpu_custom_call" | custom-call | flops 13287555072 | bytes 41943040 | tf_op jit(solution)/shard_map/moe_exchange/pallas_call | solution.py:490
  168.1 0.7 slice_bitcast_fusion.2
  168.8 2.2 %fusion = (bf16[1,352,2048]{2,1,0:T(8,128)(2,1)}, bf16[1,2048,352]{1,2,0:T(8,128)(2,1)}, bf16[1,2048,352]{1,2,0:T(8,128)(2,1)}) fusion(bf16[3,352,2048]{2,1,0:T(8,128)(2,1)S(1)} %get-tuple-element.11), kind=kLoop, calls=%fused_computation.4 | loop fusion | bytes 8650752 | tf_op jit(solution)/shard_map/slice | solution.py:553
  171.0 0.6 copy.14

commit v4 on v3

--- a/solution.py
+++ b/solution.py
@@ -10,7 +10,7 @@
 F32 = jnp.float32
 BF16 = jnp.bfloat16
 CHUNKS = 8
-AHEAD = 5
+AHEAD = 7
 CORES = 2
 NEAR = 1
 NEAR_AT = (3, 9)

time: 173 us -> 174 us (level)
  no operation moved by 1% of the time
where the time goes in v4:
time: 174 us; the launch traced here: 171 us
  Pallas kernels  167 us (96%)
  local copies, waits for them, and re-layouts  3.52 us (2%)
    pallas_call x1, Pallas kernels, run_kernel(): pl.pallas_call(functools.partial(moe_kernel, E, T, C, NC, GL), out_shape=...  167 us

profile of v4, /device:TPU:32, one launch (start us, length us, event | category | flops | bytes accessed | tf_op | source)
XLA Modules:
  0.0 171.4 jit_solution(16542417710044552528)
XLA Ops:
  0.6 167.2 %moe_exchange.1 = (bf16[3,352,2048]{2,1,0:T(8,128)(2,1)S(1)}, bf16[2,128,512]{2,1,0:T(8,128)(2,1)S(1)}, f32[6,128]{1,0:T(8,128)S(1)}) custom-call(bf16[128,512]{1,0:T(8,128)(2,1)} %tok_hbm.1, bf16[128,512]{1,0:T(8,128)(2,1)} %grad_hbm.1, f32[6,128]{1,0:T(8,128)} %bitcast.30, s32[6,128]{1,0:T(8,128)} %bitcast.31, bf16[352,2048]{1,0:T(8,128)(2,1)} %bitcast.27, ...), custom_call_target="tpu_custom_call" | custom-call | flops 13287555072 | bytes 41943040 | tf_op jit(solution)/shard_map/moe_exchange/pallas_call | solution.py:490
  167.9 0.7 slice_bitcast_fusion.2
  168.6 2.2 %fusion = (bf16[1,352,2048]{2,1,0:T(8,128)(2,1)}, bf16[1,2048,352]{1,2,0:T(8,128)(2,1)}, bf16[1,2048,352]{1,2,0:T(8,128)(2,1)}) fusion(bf16[3,352,2048]{2,1,0:T(8,128)(2,1)S(1)} %get-tuple-element.11), kind=kLoop, calls=%fused_computation.4 | loop fusion | bytes 8650752 | tf_op jit(solution)/shard_map/slice | solution.py:553
  170.8 0.6 copy.14
